TPU v7x, 256 devices: a whole 4x4x8 slice. The times are simulated.
256 devices in a mesh: mix: 4 (over z_hi), fsdp: 4 (over x), tile: 16 (over z_lo, y, core).
Axes of the slice: x: 4, y: 4, z: 8 (z_hi: 4, z_lo: 2; z = z_hi * 2 + z_lo), core: 2. Of those that a mesh axis runs over, the one named last changes fastest.
Arguments:
- video: bfloat16 [16, 64, 8, 8, 256], P(('mix', 'fsdp'), 'tile'), parts along dimension 0
- conv_weight: bfloat16 [1024, 6912], P(('mix', 'fsdp')), parts along dimension 0, may hold values from -0.078125 to 0.078125
- down_weight: bfloat16 [1024, 2304], P(('mix', 'fsdp')), parts along dimension 0, may hold values from -0.125 to 0.125
- out_grad: bfloat16 [16, 64, 4, 4, 256], P(('mix', 'fsdp'), 'tile'), parts along dimension 0, may hold values from -6 to 6
- clip_bucket: int32 [16], P(('mix', 'fsdp')), parts along dimension 0, may hold values from 0 to 3
- start_frame: int32 [16], P(('mix', 'fsdp')), parts along dimension 0, may hold values from 0 to 32
- bucket_res: int32 [4, 2], replicated, may hold values from 4 to 8, as said below
Outputs:
- down: bfloat16 [16, 64, 4, 4, 256], P(('mix', 'fsdp'), 'tile'), parts along dimension 0
- video_grad: bfloat16 [16, 64, 8, 8, 256], P(('mix', 'fsdp'), 'tile'), parts along dimension 0
- conv_weight_grad: float32 [1024, 6912], P(('mix', 'fsdp')), parts along dimension 0
- down_weight_grad: float32 [1024, 2304], P(('mix', 'fsdp')), parts along dimension 0
There are 4 independent parts, one for each index of `mix`. A program takes and returns all parts, laid end to end along the dimension named above; an argument that names none is the same for every part. Nothing has to cross between parts.
Inputs may be any that keep to these rules, and one draw needn't show every extreme that they name: `start_frame`: frames before it are padding. `bucket_res`: valid rows (column 0) and columns (column 1) per bucket; no two buckets have the same pair.
All inputs are finite; a program needn't handle non-finite values.
Results may differ from a plain program's by a relative error of at most 0.0051.
Values may be sent and summed in bfloat16 or wider, within the bound.
No kernel may reach another device: no remote copies, remote signals or barrier semaphores. Data moves between devices by JAX's collectives and lax.ppermute only.
A program may use at most 128 MiB of HBM per device.

v0:
```python
import jax
import jax.numpy as jnp
from jax import lax
from jax.sharding import PartitionSpec as P

GROUPS = 32


EPSILON = 1e-06


def shifted(block, axis, distance):
    devices = range(lax.axis_size(axis))
    route = [(i - distance, i) for i in devices if i - distance in devices]
    return lax.ppermute(block, axis, route)


def valid_mask(clip_bucket, start_frame, bucket_res, first_frame, frame_count, side_cells):
    bucket_ids = jnp.arange(bucket_res.shape[0], dtype=jnp.int32)
    picked = (clip_bucket[:, None] == bucket_ids[None, :]).astype(jnp.int32)
    limits = jnp.sum(picked[:, :, None] * bucket_res[None, :, :], axis=1)
    frame_ids = first_frame + jnp.arange(frame_count, dtype=jnp.int32)
    positions = jnp.arange(side_cells, dtype=jnp.int32)
    in_time = frame_ids[None, :] >= start_frame[:, None]
    in_rows = positions[None, :] < limits[:, 0:1]
    in_cols = positions[None, :] < limits[:, 1:2]
    inside = in_time[:, :, None, None] & in_rows[:, None, :, None] & in_cols[:, None, None, :]
    return (inside.astype(jnp.float32)[..., None], limits)


def time_group(padded, tap_time, out_frames, side_cells, flipped):
    channel_count = padded.shape[-1]
    time_start = 2 - tap_time if flipped else tap_time
    layers = []
    for tap_row in range(3):
        for tap_col in range(3):
            row_start = 2 - tap_row if flipped else tap_row
            col_start = 2 - tap_col if flipped else tap_col
            window = padded[
                :,
                time_start : time_start + out_frames,
                row_start : row_start + side_cells,
                col_start : col_start + side_cells,
                :,
            ]
            layers.append(window.reshape(-1, channel_count))
    return jnp.stack(layers)


def stride_taps(padded, side_cells):
    channel_count = padded.shape[-1]
    layers = []
    for tap_row in range(3):
        for tap_col in range(3):
            window = padded[
                :, :, tap_row : tap_row + side_cells : 2, tap_col : tap_col + side_cells : 2, :
            ]
            layers.append(window.reshape(-1, channel_count))
    return jnp.stack(layers)


def weight_terms(grad_rows, slabs, cot_rows, hidden_padded, frame_count, side_cells):
    out_rows = grad_rows.shape[1]
    down_term = lax.dot_general(
        grad_rows, slabs, (((0,), (1,)), ((), ())), preferred_element_type=jnp.float32
    ).reshape(out_rows, -1)
    conv_parts = []
    for tap_time in range(3):
        group = time_group(hidden_padded, tap_time, frame_count, side_cells, False)
        conv_parts.append(
            lax.dot_general(
                cot_rows, group, (((0,), (1,)), ((), ())), preferred_element_type=jnp.float32
            )
        )
    conv_term = jnp.concatenate(conv_parts, axis=1).reshape(out_rows, -1)
    return (conv_term, down_term)


def transpose_conv(grad_padded, conv_weight, out_frames, side_cells):
    channel_count = grad_padded.shape[-1]
    row_total = grad_padded.shape[0] * out_frames * side_cells * side_cells
    initial = jnp.zeros((row_total, channel_count), jnp.float32)
    running = initial
    weight_panel = lax.all_gather(conv_weight, "fsdp", axis=0, tiled=True)
    panel_rows = weight_panel.shape[0]
    panel = weight_panel.reshape(panel_rows, 27, channel_count)
    for tap_time in range(3):
        group = time_group(grad_padded, tap_time, out_frames, side_cells, True)
        running = running + lax.dot_general(
            group,
            panel[:, 9 * tap_time : 9 * tap_time + 9, :],
            (((0, 2), (1, 0)), ((), ())),
            preferred_element_type=jnp.float32,
        )
    return running


def shards(video, conv_weight, down_weight, out_grad, clip_bucket, start_frame, bucket_res):
    clip_count, frame_count, side_cells, side_again, channel_count = video.shape
    half_side = side_cells // 2
    group_width = channel_count // GROUPS
    tiles = lax.axis_size("tile")
    mask, limits = valid_mask(
        clip_bucket,
        start_frame,
        bucket_res,
        lax.axis_index("tile") * frame_count,
        frame_count,
        side_cells,
    )
    valid_count = (
        (frame_count * tiles - start_frame) * limits[:, 0] * limits[:, 1] * group_width
    ).astype(jnp.float32)
    grouped_shape = (clip_count, frame_count, side_cells, side_cells, GROUPS, group_width)
    summed_axes = (1, 2, 3, 5)
    cell_weight = mask[..., None]
    grouped = video.astype(jnp.float32).reshape(grouped_shape)
    first_sum = lax.psum(jnp.sum(grouped * cell_weight, axis=summed_axes), "tile")
    centre = first_sum / valid_count[:, None]
    offset = grouped - centre[:, None, None, None, :, None]
    second_sum = lax.psum(jnp.sum(cell_weight * offset * offset, axis=summed_axes), "tile")
    spread = second_sum / valid_count[:, None]
    inverse = lax.rsqrt(spread + EPSILON)
    normed_grouped = offset * inverse[:, None, None, None, :, None]
    normed = normed_grouped.reshape(video.shape)
    hidden = (mask * jax.nn.silu(normed)).astype(jnp.bfloat16)
    past = shifted(hidden[:, frame_count - 2 :], "tile", 1)
    hidden_padded = jnp.pad(
        jnp.concatenate([past, hidden], axis=1), ((0, 0), (0, 0), (1, 1), (1, 1), (0, 0))
    )

    def conv_columns(weight_panel):
        panel = weight_panel.reshape(weight_panel.shape[0], 27, channel_count)
        summed = None
        for tap_time in range(3):
            group = time_group(hidden_padded, tap_time, frame_count, side_cells, False)
            term = lax.dot_general(
                group,
                panel[:, 9 * tap_time : 9 * tap_time + 9, :],
                (((0, 2), (1, 2)), ((), ())),
                preferred_element_type=jnp.float32,
            )
            summed = term if summed is None else summed + term
        return summed

    conv_out = conv_columns(lax.all_gather(conv_weight, "fsdp", axis=0, tiled=True))
    residual = (mask * (video.astype(jnp.float32) + conv_out.reshape(video.shape))).astype(
        jnp.bfloat16
    )
    down_slabs = stride_taps(
        jnp.pad(residual, ((0, 0), (0, 0), (0, 1), (0, 1), (0, 0))), side_cells
    )
    weight_panel = lax.all_gather(down_weight, "fsdp", axis=0, tiled=True)
    panel = weight_panel.reshape(weight_panel.shape[0], 9, channel_count)
    down_out = lax.dot_general(
        down_slabs, panel, (((0, 2), (1, 2)), ((), ())), preferred_element_type=jnp.float32
    )
    down = down_out.astype(jnp.bfloat16).reshape(
        clip_count, frame_count, half_side, half_side, channel_count
    )
    grad_flat = out_grad.reshape(-1, channel_count)
    weight_panel = lax.all_gather(down_weight, "fsdp", axis=0, tiled=True)
    panel_rows = weight_panel.shape[0]
    panel = weight_panel.reshape(panel_rows, 9, channel_count)
    tap_grads = lax.dot_general(
        grad_flat, panel, (((1,), (0,)), ((), ())), preferred_element_type=jnp.float32
    )
    spread_back = jnp.zeros(
        (clip_count, frame_count, side_cells + 1, side_cells + 1, channel_count), jnp.float32
    )
    for tap_row in range(3):
        for tap_col in range(3):
            term = tap_grads[:, tap_row * 3 + tap_col, :].reshape(
                clip_count, frame_count, half_side, half_side, channel_count
            )
            spread_back = spread_back.at[
                :, :, tap_row : tap_row + side_cells : 2, tap_col : tap_col + side_cells : 2, :
            ].add(term)
    res_grad = (mask * spread_back[:, :, :side_cells, :side_cells, :]).astype(jnp.bfloat16)
    res_flat = res_grad.reshape(-1, channel_count)
    later = shifted(res_grad[:, :2], "tile", -1)
    grad_padded = jnp.pad(
        jnp.concatenate([res_grad, later], axis=1), ((0, 0), (0, 0), (1, 1), (1, 1), (0, 0))
    )
    back_hidden = transpose_conv(grad_padded, conv_weight, frame_count, side_cells).reshape(
        video.shape
    )
    gate_value = jax.nn.sigmoid(normed)
    pushed = mask * back_hidden * gate_value * (1.0 + normed * (1.0 - gate_value))
    pushed_grouped = pushed.reshape(grouped_shape)
    push_sum, pair_sum = lax.psum(
        (
            jnp.sum(pushed_grouped, axis=summed_axes),
            jnp.sum(pushed_grouped * normed_grouped, axis=summed_axes),
        ),
        "tile",
    )
    mean_push = push_sum / valid_count[:, None]
    mean_pair = pair_sum / valid_count[:, None]
    through_norm = inverse[:, None, None, None, :, None] * (
        pushed_grouped
        - mean_push[:, None, None, None, :, None]
        - normed_grouped * mean_pair[:, None, None, None, :, None]
    )
    video_grad = (mask * through_norm.reshape(video.shape) + res_grad.astype(jnp.float32)).astype(
        jnp.bfloat16
    )
    conv_term, down_term = weight_terms(
        grad_flat, down_slabs, res_flat, hidden_padded, frame_count, side_cells
    )
    conv_share, down_share = (
        lax.psum_scatter(conv_term, ("fsdp", "tile"), scatter_dimension=0, tiled=True),
        lax.psum_scatter(down_term, ("fsdp", "tile"), scatter_dimension=0, tiled=True),
    )
    conv_weight_grad, down_weight_grad = (
        lax.all_gather(conv_share, "tile", axis=0, tiled=True),
        lax.all_gather(down_share, "tile", axis=0, tiled=True),
    )
    return (down, video_grad, conv_weight_grad, down_weight_grad)


def solution(mesh):
    placed = (
        P(("mix", "fsdp"), "tile", None, None, None),
        P(("mix", "fsdp"), None),
        P(("mix", "fsdp"), None),
        P(("mix", "fsdp"), "tile", None, None, None),
        P(("mix", "fsdp")),
        P(("mix", "fsdp")),
        P(),
    )
    return jax.shard_map(
        shards,
        mesh=mesh,
        in_specs=placed,
        out_specs=(
            P(("mix", "fsdp"), "tile", None, None, None),
            P(("mix", "fsdp"), "tile", None, None, None),
            P(("mix", "fsdp"), None),
            P(("mix", "fsdp"), None),
        ),
        check_vma=False,
    )
```

profile of v0, /device:TPU:1, one launch (start us, length us, event | category | flops | bytes accessed | tf_op | source)
XLA Modules:
  0.0 811.9 jit_solution(14755539417623536898)
XLA Ops:
  14.8 29.8 %psum.28 = f32[1,32]{1,0:T(1,128)S(1)} all-reduce(f32[1,32]{1,0:T(1,128)S(1)} %bitcast.287), channel_id=1, replica_groups=mesh['mix'=4,'fsdp'=4,'tile'=16] {'tile'}, use_global_device_ids=true, to_apply=%region_3.0 | all-reduce | flops 32 | bytes 256 | tf_op jit(solution)/shard_map/psum | solution.py:118
  44.8 1.6 copy.274
  60.7 4.6 collective-permute-start.1
  65.3 26.2 %psum.29 = f32[1,32]{1,0:T(1,128)S(1)} all-reduce(f32[1,32]{1,0:T(1,128)S(1)} %bitcast.285), channel_id=1, replica_groups=mesh['mix'=4,'fsdp'=4,'tile'=16] {'tile'}, use_global_device_ids=true, to_apply=%region_6.7 | all-reduce | flops 32 | bytes 256 | tf_op jit(solution)/shard_map/psum | solution.py:121
  96.6 5.0 copy.270
  101.6 1.9 convolution_bitcast_fusion
  105.6 1.5 fusion.47
  112.5 29.0 %all-reduce.6 = (f32[1,32]{1,0:T(1,128)}, f32[1,32]{1,0:T(1,128)}) all-reduce(f32[1,32]{1,0:T(1,128)} %bitcast.284, f32[1,32]{1,0:T(1,128)} %bitcast.286), channel_id=1, replica_groups=mesh['mix'=4,'fsdp'=4,'tile'=16] {'tile'}, use_global_device_ids=true, to_apply=%region_21.22 | all-reduce | flops 64 | bytes 512 | tf_op jit(solution)/shard_map/psum | solution.py:191
  145.6 1.4 sub.72
  147.0 1.9 fusion.29
  148.9 1.9 collective-permute-start
  160.8 2.0 fusion.54
  162.8 2.0 fusion.53
  164.8 2.1 fusion.52
  167.6 1.9 fusion.55
  170.2 4.5 pad_maximum_fusion
  176.5 584.0 %all-reduce.9.cloned.1.call-done = (f32[256,6912]{0,1:T(8,128)}, f32[256,2304]{0,1:T(8,128)}) async-done(((f32[256,6912]{0,1:T(8,128)}, f32[256,2304]{0,1:T(8,128)}), (f32[256,6912]{0,1:T(8,128)}, f32[256,2304]{0,1:T(8,128)})) %all-reduce.9.cloned.1.call-update) | async-done | bytes 9437200
  760.5 3.0 dynamic-slice_bitcast_fusion
  763.5 2.0 copy.290
  765.5 1.7 fusion.4
  767.8 1.6 dynamic-slice_bitcast_fusion.1
  769.8 19.2 %all-gather.1 = f32[16,4,2304]{2,1,0:T(4,128)S(1)} all-gather(f32[1,4,2304]{2,1,0:T(4,128)S(1)} %copy.291), channel_id=1, replica_groups=mesh['mix'=4,'fsdp'=4,'tile'=16] {'tile'}, dimensions={0}, use_global_device_ids=true | all-gather | bytes 626688 | tf_op jit(solution)/shard_map/all_gather | solution.py:217
  790.0 12.6 %all-gather.10.cloned.1.call-done = f32[16,4,6912]{2,1,0:T(4,128)} async-done(((f32[1,4,6912]{2,1,0:T(4,128)}), f32[16,4,6912]{2,1,0:T(4,128)}) %all-gather.10.cloned.1.call-update) | async-done | bytes 1769488 | tf_op jit(solution)/shard_map/all_gather | solution.py:216
  802.5 2.8 reshape.347
  (246 shorter events, 49.6 us)
Async XLA Ops:
  7.2 1.8 copy-start.19
  7.2 3.2 copy-start.26
  7.2 6.0 copy-start.6
  7.2 37.6 %all-gather.8.cloned.1.call-start = ((), (), s32[]{:S(2)}) async-start(), calls=%async_computation.1 | async-start | bytes 1474560 | tf_op jit(solution)/shard_map/all_gather | solution.py:153
  7.9 88.7 %all-gather.6.cloned.1.call-start = ((), (), s32[]{:S(2)}) async-start(), calls=%async_computation | async-start | bytes 4423680 | tf_op jit(solution)/shard_map/all_gather | solution.py:146
  8.7 751.8 %all-reduce.9.cloned.1.call-start = ((), (), s32[]{:S(2)}) async-start(), calls=%async_computation.3 | async-start | bytes 18874368
  9.0 37.4 %copy-start.15 = (bf16[64,256,1]{1,0,2:T(8,128)(2,1)}, bf16[64,256,1]{1,0,2:T(8,128)(2,1)S(1)}, u32[]{:S(2)}) copy-start(bf16[64,256,1]{1,0,2:T(8,128)(2,1)S(1)} %reshape.354) | copy-start | bytes 98308
  44.8 15.6 %copy-start.20 = (f32[256]{0:T(256)}, f32[256]{0:T(256)S(1)}, u32[]{:S(2)}) copy-start(f32[256]{0:T(256)S(1)} %sub.66) | copy-start | bytes 3076
  46.4 1.0 copy-start
  60.5 33.1 %copy-start.1 = (bf16[1,4,8,8,256]{4,3,2,1,0:T(8,128)(2,1)}, bf16[1,4,8,8,256]{4,3,2,1,0:T(8,128)(2,1)S(1)}, u32[]{:S(2)}) copy-start(bf16[1,4,8,8,256]{4,3,2,1,0:T(8,128)(2,1)S(1)} %get-tuple-element.86) | copy-start | bytes 393220
  60.7 31.6 %collective-permute-start.1 = (bf16[1,2,8,8,256]{4,3,2,1,0:T(8,128)(2,1)S(1)}, bf16[1,2,8,8,256]{4,3,2,1,0:T(8,128)(2,1)S(1)}, u32[]{:S(2)}, u32[]{:S(2)}) collective-permute-start(bf16[1,2,8,8,256]{4,3,2,1,0:T(8,128)(2,1)S(1)} %slice.406), channel_id=1, source_target_pairs={{1,0},{2,1},{3,2},{4,3},{5,4},{6,5},{7,6},{8,7},{9,8},{10,9},{11,1... | collective-permute-start | bytes 196616 | tf_op jit(solution)/shard_map/ppermute | solution.py:15
  93.5 1.0 copy-start.24
  95.5 1.1 copy-start.9
  101.6 1.9 copy-start.23
  103.5 1.3 copy-start.10
  148.9 3.2 collective-permute-start
  155.2 1.0 copy-start.4
  155.2 1.0 copy-start.8
  156.2 4.6 copy-start.2
  160.8 2.0 copy-start.13
  162.8 2.0 copy-start.5
  167.6 1.9 copy-start.14
  167.6 2.5 copy-start.3
  174.6 627.9 %all-gather.10.cloned.1.call-start = ((), (), s32[]{:S(2)}) async-start(), calls=%async_computation.2 | async-start | bytes 1880064 | tf_op jit(solution)/shard_map/all_gather | solution.py:216
  (10 other events, 8.6 us)
Sparse Core Ops, SparseCore 0:
  9.8 28.5 all-gather.7
  40.2 47.8 all-gather.5
  174.7 585.7 all-reduce.8
  765.6 36.9 all-gather.9
where the time goes:
time: 813 us; the launch traced here: 812 us
  waiting for transfers between devices  599 us (74%)
  blocking collectives  104 us (13%)
  local copies, waits for them, and re-layouts  42.8 us (5%)
  other arithmetic  26.2 us (3%)
  between operations  18.3 us (2%)
  matrix products  14.4 us (2%)
    unnamed x5, waiting for transfers between devices  585 us
    psum x1, blocking collectives, shards(): lax.psum(jnp.sum(grouped * cell_weight, axis=summed_axes), 'tile')  29.8 us
    psum x1, blocking collectives, shards(): lax.psum((jnp.sum(pushed_grouped, axis=summed_axes), jnp.sum(pushed_group...  29 us
    psum x1, blocking collectives, shards(): lax.psum(jnp.sum(cell_weight * offset * offset, axis=summed_axes), 'tile')  26.2 us
    unnamed x119, local copies, waits for them, and re-layouts  20.2 us
    all_gather x1, blocking collectives, shards(): lax.all_gather(down_share, 'tile', axis=0, tiled=True)  19.2 us
  transfers between devices with their start and end apart: 6, of which 3 were waited for; matrix products, arithmetic and copies ran while one was open for 3% of the time, Pallas kernels for 0%

commit v1 on v0

--- a/solution.py
+++ b/solution.py
@@ -13,6 +13,11 @@
     devices = range(lax.axis_size(axis))
     route = [(i - distance, i) for i in devices if i - distance in devices]
     return lax.ppermute(block, axis, route)
+
+
+def everywhere(block, axis):
+    copies = jnp.broadcast_to(block[None], (lax.axis_size(axis),) + block.shape)
+    return lax.all_to_all(copies, axis, 0, 0, tiled=True)
 
 
 def valid_mask(clip_bucket, start_frame, bucket_res, first_frame, frame_count, side_cells):
@@ -115,11 +120,22 @@
     summed_axes = (1, 2, 3, 5)
     cell_weight = mask[..., None]
     grouped = video.astype(jnp.float32).reshape(grouped_shape)
-    first_sum = lax.psum(jnp.sum(grouped * cell_weight, axis=summed_axes), "tile")
-    centre = first_sum / valid_count[:, None]
+    cells_per_frame = limits[:, 0] * limits[:, 1] * group_width
+    tile_starts = jnp.arange(tiles, dtype=jnp.int32)[:, None] * frame_count
+    tile_frames = jnp.clip(tile_starts + frame_count - start_frame[None, :], 0, frame_count)
+    tile_counts = (tile_frames * cells_per_frame[None, :]).astype(jnp.float32)[:, :, None]
+    own_count = jnp.sum(mask, axis=(1, 2, 3, 4))[:, None] * group_width
+    own_sum = jnp.sum(grouped * cell_weight, axis=summed_axes)
+    own_mean = own_sum / jnp.maximum(own_count, 1.0)
+    own_offset = grouped - own_mean[:, None, None, None, :, None]
+    own_square = jnp.sum(cell_weight * own_offset * own_offset, axis=summed_axes)
+    stats = everywhere(jnp.stack([own_sum, own_square]), "tile")
+    tile_sums = stats[:, 0]
+    centre = jnp.sum(tile_sums, axis=0) / valid_count[:, None]
+    tile_drift = tile_sums / jnp.maximum(tile_counts, 1.0) - centre[None]
+    second_sum = jnp.sum(stats[:, 1] + tile_counts * tile_drift * tile_drift, axis=0)
+    spread = second_sum / valid_count[:, None]
     offset = grouped - centre[:, None, None, None, :, None]
-    second_sum = lax.psum(jnp.sum(cell_weight * offset * offset, axis=summed_axes), "tile")
-    spread = second_sum / valid_count[:, None]
     inverse = lax.rsqrt(spread + EPSILON)
     normed_grouped = offset * inverse[:, None, None, None, :, None]
     normed = normed_grouped.reshape(video.shape)
@@ -188,13 +204,16 @@
     gate_value = jax.nn.sigmoid(normed)
     pushed = mask * back_hidden * gate_value * (1.0 + normed * (1.0 - gate_value))
     pushed_grouped = pushed.reshape(grouped_shape)
-    push_sum, pair_sum = lax.psum(
-        (
-            jnp.sum(pushed_grouped, axis=summed_axes),
-            jnp.sum(pushed_grouped * normed_grouped, axis=summed_axes),
+    pushes = everywhere(
+        jnp.stack(
+            [
+                jnp.sum(pushed_grouped, axis=summed_axes),
+                jnp.sum(pushed_grouped * normed_grouped, axis=summed_axes),
+            ]
         ),
         "tile",
     )
+    push_sum, pair_sum = jnp.sum(pushes, axis=0)
     mean_push = push_sum / valid_count[:, None]
     mean_pair = pair_sum / valid_count[:, None]
     through_norm = inverse[:, None, None, None, :, None] * (
@@ -205,17 +224,18 @@
     video_grad = (mask * through_norm.reshape(video.shape) + res_grad.astype(jnp.float32)).astype(
         jnp.bfloat16
     )
+    parts = lax.axis_size("fsdp") * tiles
     conv_term, down_term = weight_terms(
         grad_flat, down_slabs, res_flat, hidden_padded, frame_count, side_cells
     )
-    conv_share, down_share = (
-        lax.psum_scatter(conv_term, ("fsdp", "tile"), scatter_dimension=0, tiled=True),
-        lax.psum_scatter(down_term, ("fsdp", "tile"), scatter_dimension=0, tiled=True),
-    )
-    conv_weight_grad, down_weight_grad = (
-        lax.all_gather(conv_share, "tile", axis=0, tiled=True),
-        lax.all_gather(down_share, "tile", axis=0, tiled=True),
-    )
+    conv_width = conv_term.shape[1]
+    terms = jnp.concatenate([conv_term, down_term], axis=1).astype(jnp.bfloat16)
+    terms = terms.reshape(parts, -1, terms.shape[1])
+    exchanged = lax.all_to_all(terms, ("fsdp", "tile"), 0, 0, tiled=True)
+    share = jnp.sum(exchanged.astype(jnp.float32), axis=0).astype(jnp.bfloat16)
+    rows = lax.all_gather(share, "tile", axis=0, tiled=True)
+    conv_weight_grad = rows[:, :conv_width].astype(jnp.float32)
+    down_weight_grad = rows[:, conv_width:].astype(jnp.float32)
     return (down, video_grad, conv_weight_grad, down_weight_grad)
 
 

time: 813 us -> 282 us (0.35)
  waiting for transfers between devices: 599 us -> 69.9 us
  blocking collectives: 104 us -> 77.2 us
  other arithmetic: 26.2 us -> 37 us
  local copies, waits for them, and re-layouts: 42.8 us -> 52.9 us
    unnamed x5 -> x3, waiting for transfers between devices: 585 us -> 1.39 us
    psum x3 -> x0, blocking collectives: 85 us -> none  [the longest x1 29.8 us: shards(): lax.psum(jnp.sum(grouped * cell_weight, axis=summed_axes), 'tile')]
    all_to_all x0 -> x2, blocking collectives: none -> 77.2 us  [the longest x1 65.4 us: shards(): exchanged = lax.all_to_all(terms, ('fsdp', 'tile'), 0, 0, tiled=True)]
    all_gather x1, waiting for transfers between devices: 0.02 us -> 22.1 us  [shards(): weight_panel = lax.all_gather(down_weight, 'fsdp', axis=0, tiled=True)]
    all_gather x1, waiting for transfers between devices: 12.6 us -> 32.8 us  [shards(): rows = lax.all_gather(share, 'tile', axis=0, tiled=True)]
    all_gather x1 -> x0, blocking collectives: 19.2 us -> none  [shards(): lax.all_gather(down_share, 'tile', axis=0, tiled=True)]
    concatenate x0 -> x3, local copies, waits for them, and re-layouts: none -> 12.5 us  [the longest x2 8.42 us: shards(): terms = jnp.concatenate([conv_term, down_term], axis=1).astype(jnp.bfloat16)]
    all_gather x1, waiting for transfers between devices: 0.01 us -> 10.1 us  [shards(): lax.all_gather(conv_weight, 'fsdp', axis=0, tiled=True)]
  transfers between devices with their start and end apart: 6 -> 6, of which waited for: 3 -> 5; matrix products, arithmetic and copies ran while one was open for 3% -> 10% of each run, Pallas kernels for 0% -> 0%
where the time goes in v1:
time: 282 us; the launch traced here: 281 us
  blocking collectives  77.2 us (27%)
  waiting for transfers between devices  69.9 us (25%)
  local copies, waits for them, and re-layouts  52.9 us (19%)
  other arithmetic  37 us (13%)
  between operations  19.6 us (7%)
  starting transfers between devices  12.8 us (5%)
  matrix products  11.6 us (4%)
    all_to_all x1, blocking collectives, shards(): exchanged = lax.all_to_all(terms, ('fsdp', 'tile'), 0, 0, tiled=True)  65.4 us
    all_gather x1, waiting for transfers between devices, shards(): rows = lax.all_gather(share, 'tile', axis=0, tiled=True)  32.8 us
    all_gather x1, waiting for transfers between devices, shards(): weight_panel = lax.all_gather(down_weight, 'fsdp', axis=0, tiled=True)  22.1 us
    scatter-add x9, other arithmetic, shards(): spread_back = spread_back.at[:, :, tap_row:tap_row + side_cells:2, tap_co...  11.9 us
    all_to_all x1, blocking collectives, everywhere(): return lax.all_to_all(copies, axis, 0, 0, tiled=True)  11.8 us
    unnamed x105, local copies, waits for them, and re-layouts  11.6 us
    all_gather x1, waiting for transfers between devices, shards(): lax.all_gather(conv_weight, 'fsdp', axis=0, tiled=True)  10.1 us
    concatenate x2, local copies, waits for them, and re-layouts, shards(): terms = jnp.concatenate([conv_term, down_term], axis=1).astype(jnp.bfloat16)  8.42 us
  transfers between devices with their start and end apart: 6, of which 5 were waited for; matrix products, arithmetic and copies ran while one was open for 10% of the time, Pallas kernels for 0%

profile of v1, /device:TPU:1, one launch (start us, length us, event | category | flops | bytes accessed | tf_op | source)
XLA Modules:
  0.0 281.0 jit_solution(5154194766792109534)
XLA Ops:
  16.3 22.1 %all-gather.7.cloned.1.call-done = bf16[256,2304]{1,0:T(8,128)(2,1)} async-done(((bf16[64,2304]{1,0:T(8,128)(2,1)}), bf16[256,2304]{1,0:T(8,128)(2,1)}) %all-gather.7.cloned.1.call-update) | async-done | bytes 1179664 | tf_op jit(solution)/shard_map/all_gather | solution.py:169
  38.4 1.6 copy.459
  54.9 8.1 %all-to-all-start = ((f32[16,2,1,32]{3,2,1,0:T(1,128)}), f32[16,2,1,32]{3,2,1,0:T(1,128)S(1)}, u32[]{:S(2)}, u32[]{:S(2)}) async-start(f32[16,2,1,32]{3,2,1,0:T(1,128)} %broadcast_in_dim.47), calls=%async_computation | async-start | bytes 32768 | tf_op jit(solution)/shard_map/all_to_all | solution.py:20
  64.4 2.2 collective-permute-start.1
  66.6 2.2 all-to-all-done
  78.0 10.1 %all-gather.5.cloned.1.call-done = bf16[256,6912]{1,0:T(8,128)(2,1)} async-done(((bf16[64,6912]{1,0:T(8,128)(2,1)}), bf16[256,6912]{1,0:T(8,128)(2,1)}) %all-gather.5.cloned.1.call-update) | async-done | bytes 3538960 | tf_op jit(solution)/shard_map/all_gather | solution.py:162
  88.1 5.0 %copy.455 = bf16[256,6912]{0,1:T(8,128)(2,1)S(1)} copy(bf16[256,6912]{1,0:T(8,128)(2,1)} %all-gather.5.cloned.1.call-done) | data formatting | bytes 7077888 | tf_op jit(solution)/shard_map/all_gather | solution.py:162
  93.1 1.9 convolution_bitcast_fusion
  95.5 1.8 fusion.4
  105.0 11.8 %all_to_all.15 = f32[16,2,1,32]{3,2,1,0:T(1,128)} all-to-all(f32[16,2,1,32]{3,2,1,0:T(1,128)S(1)} %broadcast_in_dim.111), channel_id=1, replica_groups=mesh['mix'=4,'fsdp'=4,'tile'=16] {'tile'}, dimensions={0} | all-to-all | bytes 8192 | tf_op jit(solution)/shard_map/all_to_all | solution.py:20
  124.3 1.9 fusion.32
  126.2 2.5 collective-permute-start
  140.0 1.6 convolution_convert_fusion.2
  141.5 1.5 convolution_convert_fusion.3
  144.1 1.5 fusion
  145.6 3.4 %copy.477 = bf16[256,9,256]{2,1,0:T(8,128)(2,1)S(1)} copy(bf16[256,9,256]{0,2,1:T(8,128)(2,1)} %fusion) | data formatting | bytes 2359296 | tf_op jit(solution)/shard_map/dot_general | solution.py:69
  149.0 1.7 concatenate.59
  150.7 1.8 pad_maximum_fusion.1
  152.5 4.1 %copy.476 = bf16[256,27,256]{2,1,0:T(8,128)(2,1)} copy(bf16[256,27,256]{2,0,1:T(8,128)(2,1)S(1)} %pad_maximum_fusion.1) | data formatting | bytes 7077888 | tf_op jit(solution)/shard_map/concatenate | solution.py:80
  156.6 6.8 %concatenate.58 = bf16[64,4,6912]{2,1,0:T(4,128)(2,1)S(1)} reshape(bf16[256,27,256]{2,1,0:T(8,128)(2,1)} %copy.476) | data formatting | bytes 7077888 | tf_op jit(solution)/shard_map/concatenate | solution.py:232
  163.3 3.4 %pad_maximum_fusion = bf16[64,4,9216]{2,1,0:T(4,128)(2,1)S(1)} fusion(bf16[64,4,2304]{2,1,0:T(4,128)(2,1)} %concatenate.59, bf16[64,4,6912]{2,1,0:T(4,128)(2,1)S(1)} %concatenate.58), kind=kLoop, calls=%fused_computation.9 | loop fusion | flops 9437184 | bytes 9437184 | tf_op jit(solution)/shard_map/concatenate | solution.py:232
  166.7 65.4 %all_to_all.16 = bf16[64,4,9216]{2,1,0:T(4,128)(2,1)} all-to-all(bf16[64,4,9216]{2,1,0:T(4,128)(2,1)S(1)} %pad_maximum_fusion), channel_id=1, replica_groups=mesh['mix'=4,'fsdp'=4,'tile'=16] {'fsdp','tile'}, dimensions={0} | all-to-all | bytes 9437184 | tf_op jit(solution)/shard_map/all_to_all | solution.py:234
  232.1 5.0 %reduce_sum.141 = bf16[4,9216]{1,0:T(4,128)(2,1)} reduce(bf16[64,4,9216]{2,1,0:T(4,128)(2,1)} %all_to_all.16, bf16[]{:T(256)} %constant.10.clone.1), dimensions={0}, to_apply=%region_22.23 | reduce | flops 2322432 | bytes 4792322 | tf_op jit(solution)/shard_map/reduce_sum | solution.py:235
  238.1 32.8 %all-gather.9.cloned.1.call-done = bf16[16,4,9216]{2,1,0:T(4,128)(2,1)} async-done(((bf16[1,4,9216]{2,1,0:T(4,128)(2,1)}), bf16[16,4,9216]{2,1,0:T(4,128)(2,1)}) %all-gather.9.cloned.1.call-update) | async-done | bytes 1179664 | tf_op jit(solution)/shard_map/all_gather | solution.py:236
  (249 shorter events, 61.4 us)
Async XLA Ops:
  7.2 2.3 copy-start.23
  7.2 5.9 %copy-start.17 = (bf16[1,4,4,4,256]{4,3,2,1,0:T(4,128)(2,1)S(1)}, bf16[1,4,4,4,256]{4,3,2,1,0:T(4,128)(2,1)}, u32[]{:S(2)}) copy-start(bf16[1,4,4,4,256]{4,3,2,1,0:T(4,128)(2,1)} %param.10) | copy-start | bytes 98308
  7.2 6.6 %copy-start.6 = (bf16[1,4,8,8,256]{4,3,2,1,0:T(8,128)(2,1)S(1)}, bf16[1,4,8,8,256]{4,3,2,1,0:T(8,128)(2,1)}, u32[]{:S(2)}) copy-start(bf16[1,4,8,8,256]{4,3,2,1,0:T(8,128)(2,1)} %param.7) | copy-start | bytes 393220
  7.2 31.2 %all-gather.7.cloned.1.call-start = ((), (), s32[]{:S(2)}) async-start(), calls=%async_computation.4 | async-start | bytes 1474560 | tf_op jit(solution)/shard_map/all_gather | solution.py:169
  7.9 80.2 %all-gather.5.cloned.1.call-start = ((), (), s32[]{:S(2)}) async-start(), calls=%async_computation.3 | async-start | bytes 4423680 | tf_op jit(solution)/shard_map/all_gather | solution.py:162
  13.1 26.9 %copy-start.15 = (bf16[64,256,1]{1,0,2:T(8,128)(2,1)}, bf16[64,256,1]{1,0,2:T(8,128)(2,1)S(1)}, u32[]{:S(2)}) copy-start(bf16[64,256,1]{1,0,2:T(8,128)(2,1)S(1)} %reshape.554) | copy-start | bytes 98308
  40.0 1.1 copy-start
  54.1 17.7 %copy-start.2 = (bf16[1,4,8,8,256]{4,3,2,1,0:T(8,128)(2,1)}, bf16[1,4,8,8,256]{4,3,2,1,0:T(8,128)(2,1)S(1)}, u32[]{:S(2)}) copy-start(bf16[1,4,8,8,256]{4,3,2,1,0:T(8,128)(2,1)S(1)} %get-tuple-element.92) | copy-start | bytes 393220
  54.9 13.9 %all-to-all-start = ((f32[16,2,1,32]{3,2,1,0:T(1,128)}), f32[16,2,1,32]{3,2,1,0:T(1,128)S(1)}, u32[]{:S(2)}, u32[]{:S(2)}) async-start(f32[16,2,1,32]{3,2,1,0:T(1,128)} %broadcast_in_dim.47), calls=%async_computation | async-start | bytes 32768 | tf_op jit(solution)/shard_map/all_to_all | solution.py:20
  63.0 207.9 %all-gather.9.cloned.1.call-start = ((), (), s32[]{:S(2)}) async-start(), calls=%async_computation.5 | async-start | bytes 1253376 | tf_op jit(solution)/shard_map/all_gather | solution.py:236
  64.4 6.1 %collective-permute-start.1 = (bf16[1,2,8,8,256]{4,3,2,1,0:T(8,128)(2,1)S(1)}, bf16[1,2,8,8,256]{4,3,2,1,0:T(8,128)(2,1)S(1)}, u32[]{:S(2)}, u32[]{:S(2)}) collective-permute-start(bf16[1,2,8,8,256]{4,3,2,1,0:T(8,128)(2,1)S(1)} %slice.428), channel_id=1, source_target_pairs={{1,0},{2,1},{3,2},{4,3},{5,4},{6,5},{7,6},{8,7},{9,8},{10,9},{11,1... | collective-permute-start | bytes 196616 | tf_op jit(solution)/shard_map/ppermute | solution.py:15
  72.7 4.6 %copy-start.18 = (bf16[9,256,256]{2,1,0:T(8,128)(2,1)}, bf16[9,256,256]{2,1,0:T(8,128)(2,1)S(1)}, u32[]{:S(2)}) copy-start(bf16[9,256,256]{2,1,0:T(8,128)(2,1)S(1)} %constant_dynamic-update-slice_fusion.45) | copy-start | bytes 3538948
  93.1 1.9 copy-start.19
  95.5 1.9 copy-start.7
  95.5 1.9 copy-start.21
  95.5 1.9 copy-start.22
  126.2 3.8 %collective-permute-start = (bf16[1,2,8,8,256]{4,3,2,1,0:T(8,128)(2,1)S(1)}, bf16[1,2,8,8,256]{4,3,2,1,0:T(8,128)(2,1)S(1)}, u32[]{:S(2)}, u32[]{:S(2)}) collective-permute-start(bf16[1,2,8,8,256]{4,3,2,1,0:T(8,128)(2,1)S(1)} %slice.410), channel_id=1, source_target_pairs={{0,1},{1,2},{2,3},{3,4},{4,5},{5,6},{6,7},{7,8},{8,9},{9,10},{10,1... | collective-permute-start | bytes 196616 | tf_op jit(solution)/shard_map/ppermute | solution.py:15
  131.8 1.1 copy-start.11
  134.0 4.6 %copy-start.3 = (bf16[1,4,8,8,256]{4,3,2,1,0:T(8,128)(2,1)S(1)}, bf16[1,4,8,8,256]{4,3,2,1,0:T(8,128)(2,1)}, u32[]{:S(2)}) copy-start(bf16[1,4,8,8,256]{4,3,2,1,0:T(8,128)(2,1)} %copy-done.2) | copy-start | bytes 393220
  134.0 4.6 %copy-start.10 = (bf16[9,256,256]{2,1,0:T(8,128)(2,1)S(1)}, bf16[9,256,256]{2,1,0:T(8,128)(2,1)}, u32[]{:S(2)}) copy-start(bf16[9,256,256]{2,1,0:T(8,128)(2,1)} %copy-done.9) | copy-start | bytes 3538948
  138.7 1.3 copy-start.12
  140.0 1.6 copy-start.5
  232.1 5.0 %copy-start.1 = (bf16[256,2304]{0,1:T(8,128)(2,1)S(1)}, bf16[256,2304]{0,1:T(8,128)(2,1)}, u32[]{:S(2)}) copy-start(bf16[256,2304]{0,1:T(8,128)(2,1)} %copy-done) | copy-start | bytes 3538948
  232.1 5.0 %copy-start.14 = (bf16[9,64,256]{2,1,0:T(8,128)(2,1)S(1)}, bf16[9,64,256]{2,1,0:T(8,128)(2,1)}, u32[]{:S(2)}) copy-start(bf16[9,64,256]{2,1,0:T(8,128)(2,1)} %copy-done.13) | copy-start | bytes 884740
  (6 other events, 5.8 us)
Sparse Core Ops, SparseCore 0:
  9.8 28.5 all-gather.6
  40.2 47.8 all-gather.4
  237.2 33.5 all-gather.8
